TPU v7x, 256 devices: a whole 4x4x8 slice. The times are simulated.
256 devices in a mesh: ctx: 16 (over x_hi, y, core), exp: 16 (over z, x_lo).
Axes of the slice: x: 4 (x_hi: 2, x_lo: 2; x = x_hi * 2 + x_lo), y: 4, z: 8, core: 2. Of those that a mesh axis runs over, the one named last changes fastest.
Arguments:
- query: bfloat16 [1024, 8192], P('ctx', 'exp'), may hold values from -7 to 7
- keys: bfloat16 [32768, 512], P('ctx'), may hold values from -9 to 9
- values: bfloat16 [32768, 512], P('ctx'), may hold values from -6 to 6
- out_weight: bfloat16 [8192, 4096], P('exp'), may hold values from -3 to 3
- residual: bfloat16 [1024, 4096], P(('ctx', 'exp')), may hold values from -6 to 6
- norm_gain: float32 [4096], replicated, may hold values from 0.1 to 1.9
- expert_ids: int32 [1024, 8], P(('ctx', 'exp')), may hold values from 0 to 31, all different within a row; in each aligned block of 4 rows (0 to 3, 4 to 7, ...) at most 2 rows name the same one
- gate_values: float32 [1024, 8], P(('ctx', 'exp')), may hold values from 0.05 to 1
- w_gate_up: bfloat16 [32, 4096, 3072], P('exp', 'ctx'), may hold values from -0.09375 to 0.09375
- w_down: bfloat16 [32, 1536, 4096], P('exp', None, 'ctx'), may hold values from -0.15625 to 0.15625
Outputs:
- layer_out: float32 [1024, 4096], P(('ctx', 'exp'))
- head_max: float32 [64], P('exp')
Inputs may be any that keep to these rules, and one draw needn't show every extreme that they name: `expert_ids`: each row names 8 different experts; in the rows of one device no expert is named more than 2 times.
All inputs are finite; a program needn't handle non-finite values.
Results may differ from a plain program's by a relative error of at most 0.018.
Values may be sent and summed in bfloat16 or wider, within the bound.
A program may use at most 192 MiB of HBM per device.

v0:
```python
import math

import jax
import jax.numpy as jnp
from jax import lax
from jax.sharding import PartitionSpec as P

D = 4096
HEADS = 64
KVH = 4
HD = 128
FF = 1536
TOP = 8
EXPERTS = 32


eps = 1e-06


def attend_block(carry_state, q_rows, k_block, v_block, q_pos):
    weighted, row_peak, row_total = carry_state
    score_scale = 1.0 / math.sqrt(q_rows.shape[1])
    scores = (
        jnp.einsum("rd,kd->rk", q_rows, k_block, preferred_element_type=jnp.float32) * score_scale
    )
    k_pos = jnp.arange(k_block.shape[0], dtype=jnp.int32)
    visible = k_pos[None, :] <= q_pos[:, None]
    masked = jnp.where(visible, scores, -1e30)
    new_peak = jnp.maximum(row_peak, jnp.max(masked, axis=1))
    weights = jnp.where(visible, jnp.exp(masked - new_peak[:, None]), 0.0)
    row_total = jnp.sum(weights, axis=1)
    weighted = jnp.dot(weights.astype(jnp.bfloat16), v_block, preferred_element_type=jnp.float32)
    return (weighted, new_peak, row_total)


def local(
    query, keys, values, out_weight, residual, norm_gain, expert_ids, gate_values, w_gate_up, w_down
):
    ctx_count = lax.axis_size("ctx")
    exp_count = lax.axis_size("exp")
    ctx_index = lax.axis_index("ctx")
    exp_index = lax.axis_index("exp")
    q_local, q_width = query.shape
    head_count = q_width // HD
    key_local = keys.shape[0]
    length = key_local * ctx_count
    slab_rows = q_local * ctx_count
    kv_index = exp_index * head_count // (HEADS // KVH)
    k_head = lax.dynamic_slice_in_dim(keys, kv_index * HD, HD, 1)
    v_head = lax.dynamic_slice_in_dim(values, kv_index * HD, HD, 1)
    q_rows = (
        query.reshape(q_local, head_count, HD).transpose(1, 0, 2).reshape(head_count * q_local, HD)
    )
    row_offsets = jnp.tile(jnp.arange(q_local, dtype=jnp.int32), head_count)
    flat_rows = head_count * q_local
    start_state = (
        jnp.zeros((flat_rows, HD), jnp.float32),
        jnp.full((flat_rows,), -1e30, jnp.float32),
        jnp.zeros((flat_rows,), jnp.float32),
    )
    q_pos = length - slab_rows + ctx_index * q_local + row_offsets
    weighted, row_peak, row_total = attend_block(
        start_state,
        q_rows,
        lax.all_gather(k_head, "ctx", axis=0, tiled=True),
        lax.all_gather(v_head, "ctx", axis=0, tiled=True),
        q_pos,
    )
    attended = (weighted / row_total[:, None]).astype(jnp.bfloat16)
    attended = (
        attended.reshape(head_count, q_local, HD)
        .transpose(1, 0, 2)
        .reshape(q_local, head_count * HD)
    )
    head_peak = jnp.max(row_peak.reshape(head_count, q_local), axis=1)
    head_max = lax.pmax(head_peak, "ctx")
    part_rows = attended
    projected = lax.psum_scatter(
        jnp.dot(part_rows, out_weight, preferred_element_type=jnp.float32),
        "exp",
        scatter_dimension=0,
        tiled=True,
    )
    state_rows = residual.astype(jnp.float32) + projected
    normed = (
        state_rows
        * lax.rsqrt(jnp.mean(state_rows * state_rows, axis=1, keepdims=True) + eps)
        * norm_gain
    ).astype(jnp.bfloat16)
    local_rows = normed.shape[0]
    slot_cap = max(2, 2 * local_rows * TOP // EXPERTS)
    slot_count = slot_cap * EXPERTS
    flat_ids = expert_ids.reshape(-1)
    onehot_ids = (flat_ids[:, None] == jnp.arange(EXPERTS, dtype=jnp.int32)[None, :]).astype(
        jnp.int32
    )
    earlier = jnp.cumsum(onehot_ids, axis=0) - onehot_ids
    slot_rank = jnp.sum(earlier * onehot_ids, axis=1)
    target = slot_rank * EXPERTS + flat_ids
    slot_table = target[None, :] == jnp.arange(slot_count, dtype=jnp.int32)[:, None]
    place_rows = jnp.any(slot_table.reshape(slot_count, local_rows, TOP), axis=2).astype(
        jnp.bfloat16
    )
    outgoing = jnp.dot(place_rows, normed, preferred_element_type=jnp.float32).astype(jnp.bfloat16)
    outgoing = outgoing.reshape(1, 1, slot_cap, EXPERTS, D)
    incoming = lax.all_to_all(
        lax.all_to_all(outgoing, "ctx", split_axis=4, concat_axis=1, tiled=True),
        "exp",
        split_axis=3,
        concat_axis=0,
        tiled=True,
    )
    expert_local = w_down.shape[0]
    d_local = w_gate_up.shape[1]
    expert_rows = incoming.reshape(-1, expert_local, d_local)
    part_rows = expert_rows
    summed = lax.psum(
        jnp.einsum("mxd,xdf->mxf", part_rows, w_gate_up, preferred_element_type=jnp.float32).astype(
            jnp.bfloat16
        ),
        "ctx",
    ).astype(jnp.float32)
    inner_units = (jax.nn.silu(summed[..., :FF]) * summed[..., FF:]).astype(jnp.bfloat16)
    expert_out = jnp.einsum(
        "mxf,xfd->mxd", inner_units, w_down, preferred_element_type=jnp.float32
    ).astype(jnp.bfloat16)
    shaped = expert_out.reshape(exp_count, ctx_count, slot_cap, expert_local, d_local)
    returned = lax.all_to_all(
        lax.all_to_all(shaped, "ctx", split_axis=1, concat_axis=4, tiled=True),
        "exp",
        split_axis=0,
        concat_axis=3,
        tiled=True,
    )
    back_rows = returned.reshape(slot_count, D)
    pick_table = (target[:, None] == jnp.arange(slot_count, dtype=jnp.int32)[None, :]).astype(
        jnp.bfloat16
    )
    per_choice = jnp.dot(pick_table, back_rows, preferred_element_type=jnp.float32).reshape(
        local_rows, TOP, D
    )
    moe_sum = jnp.sum(per_choice * gate_values[:, :, None], axis=1)
    layer_out = state_rows + moe_sum
    return (layer_out, head_max)


def solution(mesh):
    return jax.shard_map(
        local,
        mesh=mesh,
        in_specs=(
            P("ctx", "exp"),
            P("ctx", None),
            P("ctx", None),
            P("exp", None),
            P(("ctx", "exp"), None),
            P(),
            P(("ctx", "exp"), None),
            P(("ctx", "exp"), None),
            P("exp", "ctx", None),
            P("exp", None, "ctx"),
        ),
        out_specs=(P(("ctx", "exp"), None), P("exp")),
        check_vma=False,
    )
```

profile of v0, /device:TPU:225, one launch (start us, length us, event | category | flops | bytes accessed | tf_op | source)
XLA Modules:
  0.0 644.8 jit_solution(4348917887009457203)
XLA Ops:
  7.2 2.0 constant_dynamic-slice_fusion.1
  9.3 1.9 constant_dynamic-slice_fusion
  12.3 77.0 %all-gather.3.cloned.1.call-done = bf16[32768,128]{1,0:T(8,128)(2,1)} async-done(((bf16[2048,128]{1,0:T(8,128)(2,1)}), bf16[32768,128]{1,0:T(8,128)(2,1)}) %all-gather.3.cloned.1.call-update) | async-done | bytes 8388624 | tf_op jit(solution)/shard_map/all_gather | solution.py:65
  89.3 19.1 %fusion.36 = (f32[256]{0:T(256)S(1)}, f32[256,32768]{0,1:T(8,128)}) fusion(bf16[32768,128]{1,0:T(8,128)(2,1)} %all-gather.3.cloned.1.call-done, bf16[256,128]{1,0:T(8,128)(2,1)S(1)} %bitcast.61, s32[256]{0:T(256)S(1)} %add.53), kind=kOutput, calls=%fused_computation.45 | convolution fusion | flops 2181037824 | bytes 42010624 | tf_op jit(solution)/shard_map/rd,kd->rk/dot_general | solution.py:24
  108.4 15.1 %fusion.2 = f32[256]{0:T(256)S(1)} fusion(f32[256,32768]{0,1:T(8,128)} %get-tuple-element.3, f32[256]{0:T(256)S(1)} %broadcast_maximum_fusion, s32[256]{0:T(256)S(1)} %add.53), kind=kLoop, calls=%fused_computation.5 | loop fusion | flops 33554176 | bytes 33557504 | tf_op jit(solution)/shard_map/reduce_sum | solution.py:31
  123.6 44.0 %all-gather.5.cloned.1.call-done = bf16[32768,128]{1,0:T(8,128)(2,1)} async-done(((bf16[2048,128]{1,0:T(8,128)(2,1)}), bf16[32768,128]{1,0:T(8,128)(2,1)}) %all-gather.5.cloned.1.call-update) | async-done | bytes 8388624 | tf_op jit(solution)/shard_map/all_gather | solution.py:66
  167.6 17.2 %fusion.19 = bf16[256,128]{1,0:T(8,128)(2,1)S(1)} fusion(bf16[32768,128]{1,0:T(8,128)(2,1)} %all-gather.5.cloned.1.call-done, f32[256,32768]{0,1:T(8,128)} %get-tuple-element.3, f32[256]{0:T(256)S(1)} %broadcast_maximum_fusion, s32[256]{0:T(256)S(1)} %add.53, f32[256]{0:T(256)S(1)} %fusion.2), kind=kOutput, calls=%fused_computation.18 | convolution fusion | flops 2181103616 | bytes 42011648 | tf_op jit(solution)/shard_map/dot_general | solution.py:32
  184.9 4.0 fusion.22
  191.0 122.8 %all-reduce.6.cloned.1.call-done = f32[64,4096]{1,0:T(8,128)} async-done(((f32[64,4096]{1,0:T(8,128)}), f32[64,4096]{1,0:T(8,128)}) %all-reduce.6.cloned.1.call-update) | async-done | bytes 1048592
  314.9 2.1 convolution_convert_fusion
  317.0 5.3 copy.33
  322.3 5.9 reshape.120
  328.2 29.1 %all_to_all.66 = bf16[16,2,8192]{2,1,0:T(2,128)(2,1)} all-to-all(bf16[16,2,8192]{2,1,0:T(2,128)(2,1)} %reshape.120), channel_id=1, replica_groups=mesh['ctx'=16,'exp'=16] {'ctx'}, dimensions={0} | all-to-all | bytes 1048576 | tf_op jit(solution)/shard_map/all_to_all | solution.py:107
  357.2 5.9 reshape.121
  363.2 4.1 copy.34
  367.3 19.3 %all_to_all.67 = bf16[1,16,2,32,256]{4,1,2,0,3:T(8,128)(2,1)S(1)} all-to-all(bf16[1,16,2,32,256]{4,1,2,0,3:T(8,128)(2,1)} %bitcast.56), channel_id=1, replica_groups=mesh['ctx'=16,'exp'=16] {'exp'}, dimensions={3} | all-to-all | bytes 1048576 | tf_op jit(solution)/shard_map/all_to_all | solution.py:106
  386.7 1.4 copy.36
  388.0 2.0 reshape.113
  390.1 5.5 convert_bitcast_fusion
  395.6 161.1 %all-reduce.4.cloned.1.call-done = bf16[512,2,3072]{2,0,1:T(8,128)(2,1)} async-done(((bf16[512,2,3072]{2,0,1:T(8,128)(2,1)}), bf16[512,2,3072]{2,0,1:T(8,128)(2,1)}) %all-reduce.4.cloned.1.call-update) | async-done | bytes 6291472 | tf_op jit(solution)/shard_map/psum | solution.py:117
  556.7 4.5 convert_element_type.46
  561.2 2.7 fusion.12
  563.9 2.1 reshape.114
  566.0 1.3 copy.37
  567.3 18.7 %all_to_all.68 = bf16[16,16,2,2,256]{4,0,3,2,1:T(8,128)(2,1)S(1)} all-to-all(bf16[16,16,2,2,256]{4,0,3,2,1:T(8,128)(2,1)S(1)} %copy.37), channel_id=1, replica_groups=mesh['ctx'=16,'exp'=16] {'ctx'}, dimensions={1} | all-to-all | bytes 1048576 | tf_op jit(solution)/shard_map/all_to_all | solution.py:129
  587.1 2.0 reshape.117
  589.0 6.4 all-to-all-start.3
  595.6 35.4 %pmax.7 = f32[4]{0:T(128)} all-reduce(f32[4]{0:T(128)S(1)} %reduce_max.19), channel_id=1, replica_groups=mesh['ctx'=16,'exp'=16] {'ctx'}, use_global_device_ids=true, to_apply=%region_10.11 | all-reduce | flops 4 | bytes 32 | tf_op jit(solution)/shard_map/pmax | solution.py:76
  631.0 2.3 copy.40
  633.3 2.0 reshape.116
  635.3 1.4 fusion.15
  636.7 1.6 fusion.32
  (44 shorter events, 5.0 us)
Async XLA Ops:
  7.2 382.9 %copy-start = (bf16[2,256,3072]{2,1,0:T(8,128)(2,1)S(1)}, bf16[2,256,3072]{2,1,0:T(8,128)(2,1)}, u32[]{:S(2)}) copy-start(bf16[2,256,3072]{2,1,0:T(8,128)(2,1)} %param.18) | copy-start | bytes 9437188
  7.2 82.1 %all-gather.3.cloned.1.call-start = ((), (), s32[]{:S(2)}) async-start(), calls=%async_computation.4 | async-start | bytes 8912896 | tf_op jit(solution)/shard_map/all_gather | solution.py:65
  9.3 158.3 %all-gather.5.cloned.1.call-start = ((), (), s32[]{:S(2)}) async-start(), calls=%async_computation.5 | async-start | bytes 8912896 | tf_op jit(solution)/shard_map/all_gather | solution.py:66
  11.2 302.6 %all-reduce.6.cloned.1.call-start = ((), (), s32[]{:S(2)}) async-start(), calls=%async_computation.7 | async-start | bytes 2097152
  123.6 65.6 %copy-start.3 = (s32[4,8]{1,0:T(4,128)S(1)}, s32[4,8]{1,0:T(4,128)}, u32[]{:S(2)}) copy-start(s32[4,8]{1,0:T(4,128)} %param.16) | copy-start | bytes 388
  123.6 66.1 %copy-start.6 = (u32[256]{0:T(256)S(1)}, u32[256]{0:T(256)}, u32[]{:S(2)}) copy-start(u32[256]{0:T(256)} %constant.65) | copy-start | bytes 3076
  123.6 190.3 %copy-start.1 = (bf16[4,4096]{1,0:T(4,128)(2,1)S(1)}, bf16[4,4096]{1,0:T(4,128)(2,1)}, u32[]{:S(2)}) copy-start(bf16[4,4096]{1,0:T(4,128)(2,1)} %param.14) | copy-start | bytes 98308
  123.6 191.3 %copy-start.2 = (f32[4096]{0:T(1024)S(1)}, f32[4096]{0:T(1024)}, u32[]{:S(2)}) copy-start(f32[4096]{0:T(1024)} %param.15) | copy-start | bytes 49156
  188.9 367.7 %all-reduce.4.cloned.1.call-start = ((), (), s32[]{:S(2)}) async-start(), calls=%async_computation.6 | async-start | bytes 12582912 | tf_op jit(solution)/shard_map/psum | solution.py:117
  556.7 4.6 copy-start.5
  563.9 71.4 %copy-start.4 = (f32[4,8]{1,0:T(4,128)S(1)}, f32[4,8]{1,0:T(4,128)}, u32[]{:S(2)}) copy-start(f32[4,8]{1,0:T(4,128)} %param.17) | copy-start | bytes 388
  589.0 42.0 %all-to-all-start.3 = ((bf16[16,1,2,2,4096]{4,3,2,1,0:T(2,128)(2,1)}), bf16[16,1,2,2,4096]{4,3,2,1,0:T(2,128)(2,1)}, u32[]{:S(2)}, u32[]{:S(2)}) async-start(bf16[16,1,2,2,4096]{4,3,2,1,0:T(2,128)(2,1)} %reshape.117), calls=%async_computation.3 | async-start | bytes 1048576 | tf_op jit(solution)/shard_map/all_to_all | solution.py:128
Sparse Core Ops, SparseCore 0:
  10.7 78.5 all-gather.2
  92.1 75.5 all-gather.4
  189.1 124.7 all-reduce.5
  395.7 160.8 all-reduce.3
where the time goes:
time: 651 us; the launch traced here: 645 us
  waiting for transfers between devices  405 us (62%)
  blocking collectives  102 us (16%)
  matrix products  52 us (8%)
  local copies, waits for them, and re-layouts  41.2 us (6%)
  other arithmetic  22.8 us (4%)
  between operations  14.6 us (2%)
  starting transfers between devices  6.74 us (1%)
    psum x1, waiting for transfers between devices, local(): lax.psum(jnp.einsum('mxd,xdf->mxf', part_rows, w_gate_up, preferred_eleme...  161 us
    unnamed x5, waiting for transfers between devices  123 us
    all_gather x1, waiting for transfers between devices, local(): lax.all_gather(k_head, 'ctx', axis=0, tiled=True)  77 us
    all_gather x1, waiting for transfers between devices, local(): lax.all_gather(v_head, 'ctx', axis=0, tiled=True)  44 us
    pmax x1, blocking collectives, local(): head_max = lax.pmax(head_peak, 'ctx')  35.4 us
    all_to_all x1, blocking collectives, local(): lax.all_to_all(outgoing, 'ctx', split_axis=4, concat_axis=1, tiled=True)  29.1 us
    all_to_all x1, blocking collectives, local(): lax.all_to_all(lax.all_to_all(outgoing, 'ctx', split_axis=4, concat_axis=...  19.3 us
    dot_general x1, matrix products, attend_block(): jnp.einsum('rd,kd->rk', q_rows, k_block, preferred_element_type=jnp.float32)  19.1 us
  transfers between devices with their start and end apart: 5, of which 4 were waited for; matrix products, arithmetic and copies ran while one was open for 6% of the time, Pallas kernels for 0%

commit v1 on v0

v1 whole, which is shorter than its diff:
```python
import functools
import math

import jax
import jax.numpy as jnp
from jax import lax
from jax.experimental import pallas as pl
from jax.experimental.pallas import tpu as pltpu
from jax.sharding import PartitionSpec as P

HEADS = 64
KVH = 4
HD = 128
EPS = 1e-06
NEG = -1e30
MESH = pl.DeviceIdType.MESH
ANY = pl.BlockSpec(memory_space=pl.ANY)
VM = pl.BlockSpec(memory_space=pltpu.VMEM)
F32 = jnp.float32
BF16 = jnp.bfloat16
DMA = pltpu.SemaphoreType.DMA


def loop(n, body, start=0):
    def step(i, carry):
        body(i)
        return carry

    lax.fori_loop(start, n, step, 0)


def place(cn, en):
    return lax.axis_index("ctx"), lax.axis_index("exp")


def greet(targets):
    barrier = pltpu.get_barrier_semaphore()
    total = 0
    for first, last, device in targets:
        loop(
            last,
            lambda j, device=device: pl.semaphore_signal(
                barrier, inc=1, device_id=device(j), device_id_type=MESH
            ),
            start=first,
        )
        total += last - first
    pl.semaphore_wait(barrier, total)


def remote(src, dst, send, recv, device):
    return pltpu.make_async_remote_copy(
        src_ref=src,
        dst_ref=dst,
        send_sem=send,
        recv_sem=recv,
        device_id=device,
        device_id_type=MESH,
    )


def attend_kernel(cn, en, q, keys, vals, w, o, st, wother, qbuf, kbuf, vbuf, vt, sbuf, mbuf,
                  qs, qr, ws, wr, ls):
    c, e = place(cn, en)
    h = lax.rem(c, 2)
    other = c + 1 - 2 * h
    rows, width = q.shape
    heads = width // HD
    key_rows = keys.shape[0]
    half = w.shape[2] // 4
    kv = pl.multiple_of((e * heads // (HEADS // KVH)) * HD, HD)
    kcopy = pltpu.make_async_copy(keys.at[:, pl.ds(kv, HD)], kbuf, ls.at[0])
    vcopy = pltpu.make_async_copy(vals.at[:, pl.ds(kv, HD)], vbuf, ls.at[1])
    qcopy = pltpu.make_async_copy(q, qbuf.at[c], ls.at[2])
    kcopy.start()
    vcopy.start()
    qcopy.start()
    greet([(1, cn, lambda j: (lax.rem(c + j, cn), e))])

    def push(j):
        return remote(q, qbuf.at[c], qs.at[j], qr.at[c], (lax.rem(c + j, cn), e))

    loop(cn, lambda j: push(j).start(), start=1)

    def wpush(part):
        off = pl.multiple_of(part * 2 * half + (1 - h) * half, 128)
        return remote(
            w.at[:, :, pl.ds(off, half)],
            wother.at[:, :, pl.ds(part * half, half)],
            ws.at[part],
            wr.at[part],
            (other, e),
        )

    wpush(0).start()
    wpush(1).start()
    kcopy.wait()
    vcopy.wait()
    qcopy.wait()
    vt[...] = vbuf[...].astype(F32).T.astype(BF16)
    mbuf[...] = jnp.full(mbuf.shape, NEG, F32)
    cols = heads * rows
    scale = 1.0 / math.sqrt(HD)
    scale2 = scale * math.log2(math.e)
    first_q = key_rows * cn - rows * cn
    kc = min(512, key_rows)

    def one(j):
        cs = lax.rem(c + cn - j, cn)

        @pl.when(j > 0)
        def _():
            remote(q, qbuf.at[cs], qs.at[0], qr.at[cs], (cs, e)).wait_recv()

        qv = qbuf[cs]
        qcat = jnp.concatenate([qv[:, i * HD : (i + 1) * HD] for i in range(heads)], axis=0)
        for t in range(key_rows // kc):
            sbuf[t * kc : (t + 1) * kc, :] = lax.dot_general(
                kbuf[t * kc : (t + 1) * kc, :],
                qcat,
                (((1,), (1,)), ((), ())),
                preferred_element_type=F32,
            )

        @pl.when(c == cn - 1)
        def _():
            lane = lax.rem(lax.broadcasted_iota(jnp.int32, (1, cols), 1), rows)
            limit = first_q + cs * rows + lane - c * key_rows
            for t in range(key_rows // kc):
                kpos = t * kc + lax.broadcasted_iota(jnp.int32, (kc, cols), 0)
                sbuf[t * kc : (t + 1) * kc, :] = jnp.where(
                    kpos <= limit, sbuf[t * kc : (t + 1) * kc, :], NEG
                )

        m = jnp.max(sbuf[0:kc, :], axis=0, keepdims=True)
        for t in range(1, key_rows // kc):
            m = jnp.maximum(m, jnp.max(sbuf[t * kc : (t + 1) * kc, :], axis=0, keepdims=True))
        total = jnp.zeros((1, cols), F32)
        acc = jnp.zeros((HD, cols), F32)
        for t in range(key_rows // kc):
            p = jnp.exp2((sbuf[t * kc : (t + 1) * kc, :] - m) * scale2)
            total = total + jnp.sum(p, axis=0, keepdims=True)
            acc = acc + jnp.dot(
                vt[:, t * kc : (t + 1) * kc], p.astype(BF16), preferred_element_type=F32
            )
        out = acc.T.astype(BF16)
        for i in range(heads):
            o[cs, :, i * HD : (i + 1) * HD] = out[i * rows : (i + 1) * rows, :]
        ms = m * scale
        hc = cols // 2
        st[cs, 0:1, :hc] = ms[:, :hc]
        st[cs, 1:2, :hc] = ms[:, hc:]
        st[cs, 2:3, :hc] = total[:, :hc]
        st[cs, 3:4, :hc] = total[:, hc:]
        mbuf[0:1, :] = jnp.maximum(mbuf[0:1, :], ms)

    loop(cn, one)
    hc = cols // 2

    def spread(j):
        st[j, 4:5, :hc] = mbuf[0:1, :hc]
        st[j, 5:6, :hc] = mbuf[0:1, hc:]

    loop(cn, spread)
    loop(cn, lambda j: push(j).wait_send(), start=1)
    wpush(0).wait()
    wpush(1).wait()


def project_kernel(cn, en, o, st, w, out, hm, obuf, stbuf, wbuf, coef, a2, os_, or_, ss, sr, ls):
    c, e = place(cn, en)
    rows, width = o.shape[1:]
    heads = width // HD
    wcopy = pltpu.make_async_copy(w, wbuf, ls.at[0])
    ocopy = pltpu.make_async_copy(o.at[c], obuf.at[c], ls.at[1])
    scopy = pltpu.make_async_copy(st.at[c], stbuf.at[c], ls.at[2])
    wcopy.start()
    ocopy.start()
    scopy.start()
    greet([(1, cn, lambda j: (lax.rem(c + j, cn), e))])

    def opush(j):
        c2 = lax.rem(c + j, cn)
        return remote(o.at[c2], obuf.at[c], os_.at[j], or_.at[c], (c2, e))

    def spush(j):
        c2 = lax.rem(c + j, cn)
        return remote(st.at[c2], stbuf.at[c], ss.at[j], sr.at[c], (c2, e))

    def begin(j):
        spush(j).start()
        opush(j).start()

    def arrive(j):
        c2 = lax.rem(c + cn - j, cn)
        remote(st.at[c2], stbuf.at[c2], ss.at[j], sr.at[c2], (c2, e)).wait_recv()
        remote(o.at[c2], obuf.at[c2], os_.at[j], or_.at[c2], (c2, e)).wait_recv()

    loop(cn, begin, start=1)
    ocopy.wait()
    scopy.wait()
    loop(cn, arrive, start=1)
    stats = [stbuf[i] for i in range(cn)]
    top = functools.reduce(jnp.maximum, stats)
    hm[...] = top
    peak = top[0:2, :]
    weights = [jnp.exp(s[0:2, :] - peak) for s in stats]
    total = sum(wt * s[2:4, :] for wt, s in zip(weights, stats))
    coef[...] = jnp.zeros(coef.shape, F32)
    for i in range(cn):
        coef[2 * i : 2 * i + 2, :] = weights[i] / total
    turned = coef[...].T
    dup = (
        lax.broadcasted_iota(jnp.int32, (2 * rows, rows), 1)
        == lax.broadcasted_iota(jnp.int32, (2 * rows, rows), 0) // 8 * 4
        + lax.rem(lax.broadcasted_iota(jnp.int32, (2 * rows, rows), 0), 4)
    ).astype(BF16)
    for i in range(heads):
        lo = (i % (heads // 2)) * rows
        acc = jnp.zeros((rows, HD), F32)
        for k in range(cn):
            acc = acc + turned[lo : lo + rows, 2 * k + i // (heads // 2) : 2 * k + i // (heads // 2) + 1] * obuf[
                k, :, i * HD : (i + 1) * HD
            ].astype(F32)
        a2[:, i * HD : (i + 1) * HD] = jnp.dot(
            dup, acc.astype(BF16), preferred_element_type=F32
        ).astype(BF16)
    wcopy.wait()
    left = a2[...]
    n = out.shape[2]
    nc = min(256, n)
    low = lax.rem(lax.broadcasted_iota(jnp.int32, (2 * rows, nc), 0), 8) < 4

    def column(t):
        at = pl.multiple_of(t * nc, nc)
        r0 = jnp.dot(left, wbuf[:, pl.ds(at, nc)], preferred_element_type=F32)
        r1 = jnp.dot(left, wbuf[:, pl.ds(at + n, nc)], preferred_element_type=F32)
        r = jnp.where(low, r0, r1)
        for k in range(en):
            out[k, :, pl.ds(at, nc)] = r[8 * k : 8 * k + 8, :].astype(BF16)

    loop(n // nc, column)
    loop(cn, lambda j: opush(j).wait_send(), start=1)
    loop(cn, lambda j: spush(j).wait_send(), start=1)


def norm_kernel(cn, en, p, gm, residual, gain, state, x, gp, pbuf, gbuf, ps, pr, gs, gr, ls):
    c, e = place(cn, en)
    pcopy = pltpu.make_async_copy(p.at[e], pbuf.at[e], ls.at[0])
    gcopy = pltpu.make_async_copy(gm.at[e], gbuf.at[e], ls.at[1])
    pcopy.start()
    gcopy.start()
    greet([(1, en, lambda j: (c, lax.rem(e + j, en)))])

    def ppush(j):
        e2 = lax.rem(e + j, en)
        return remote(p.at[e2], pbuf.at[e], ps.at[j], pr.at[e], (c, e2))

    def gpush(j):
        e2 = lax.rem(e + j, en)
        return remote(gm.at[e2], gbuf.at[e], gs.at[j], gr.at[e], (c, e2))

    def begin(j):
        ppush(j).start()
        gpush(j).start()

    def arrive(j):
        e2 = lax.rem(e + en - j, en)
        remote(p.at[e2], pbuf.at[e2], ps.at[j], pr.at[e2], (c, e2)).wait_recv()
        remote(gm.at[e2], gbuf.at[e2], gs.at[j], gr.at[e2], (c, e2)).wait_recv()

    loop(en, begin, start=1)
    pcopy.wait()
    gcopy.wait()
    loop(en, arrive, start=1)
    gp[...] = sum(gbuf[i] for i in range(en))
    s = sum(pbuf[i].astype(F32) for i in range(en))
    n = s.shape[1]
    s0 = s[0:4, :] + residual[:, :n].astype(F32)
    s1 = s[4:8, :] + residual[:, n:].astype(F32)
    state[:, :n] = s0
    state[:, n:] = s1
    mean = (
        jnp.sum(s0 * s0, axis=1, keepdims=True) + jnp.sum(s1 * s1, axis=1, keepdims=True)
    ) * (1.0 / (2 * n))
    scale = lax.rsqrt(mean + EPS)
    n0 = s0 * scale * gain[:, :n]
    n1 = s1 * scale * gain[:, n:]
    for i in range(cn):
        part, off = (n0, i * 256) if i * 256 < n else (n1, i * 256 - n)
        x[i] = jnp.concatenate(
            [part[:, off : off + 128], part[:, off + 128 : off + 256]], axis=0
        ).astype(BF16)
    loop(en, lambda j: ppush(j).wait_send(), start=1)
    loop(en, lambda j: gpush(j).wait_send(), start=1)


def slot_gates(cn, gall, group):
    lanes = 8 * cn
    row = lax.broadcasted_iota(jnp.int32, (lanes, lanes), 0)
    col = lax.broadcasted_iota(jnp.int32, (lanes, lanes), 1)
    k = lax.broadcasted_iota(jnp.int32, (128, lanes), 0)
    which = lax.rem(lax.broadcasted_iota(jnp.int32, (128, lanes), 1) // cn, 4)
    pick = (k == 4 * group + which).astype(F32)
    spread = jnp.dot(gall, pick, preferred_element_type=F32, precision=lax.Precision.HIGHEST)
    same = row // 8 == lax.rem(col, cn)
    same_half = lax.rem(row // 4, 2) == col // (4 * cn)
    return spread, same, same_half


def expert_kernel(cn, en, x, gp, w, wother, y, gall, mid, gbuf, xbuf, wbuf, xs,
                  ms, mr, gs, gr, es, er, ps, pr, ls):
    c, e = place(cn, en)
    h = lax.rem(c, 2)
    other = c + 1 - 2 * h
    half = w.shape[2] // 4
    copies = [
        pltpu.make_async_copy(
            w.at[:, :, pl.ds(pl.multiple_of(part * 2 * half + h * half, 128), half)],
            wbuf.at[:, h, :, pl.ds(part * half, half)],
            ls.at[part],
        )
        for part in range(2)
    ]
    copies.append(pltpu.make_async_copy(wother, wbuf.at[:, 1 - h], ls.at[2]))
    xcopy = pltpu.make_async_copy(x.at[c], mid.at[c], ls.at[3])
    gcopy = pltpu.make_async_copy(gp, gbuf.at[c], ls.at[4])
    for copy in copies + [xcopy, gcopy]:
        copy.start()
    greet([
        (1, cn, lambda j: (lax.rem(c + j, cn), e)),
        (1, en, lambda j: (c, lax.rem(e + j, en))),
    ])

    def mpush(j):
        c2 = lax.rem(c + j, cn)
        return remote(x.at[c2], mid.at[c], ms.at[j], mr.at[c], (c2, e))

    def gpush(j):
        return remote(gp, gbuf.at[c], gs.at[j], gr.at[c], (lax.rem(c + j, cn), e))

    def begin(j):
        mpush(j).start()
        gpush(j).start()

    def arrive(j):
        c2 = lax.rem(c + cn - j, cn)
        remote(x.at[c2], mid.at[c2], ms.at[j], mr.at[c2], (c2, e)).wait_recv()

    loop(cn, begin, start=1)
    xcopy.wait()
    loop(cn, arrive, start=1)

    def epush(j):
        return remote(mid, xbuf.at[h, e], es.at[j], er.at[e], (c, lax.rem(e + j, en)))

    loop(en, lambda j: epush(j).start(), start=1)
    ecopy = pltpu.make_async_copy(mid, xbuf.at[h, e], ls.at[5])
    ecopy.start()
    ecopy.wait()

    def ppush(j):
        e2 = lax.rem(e + en - j, en)
        return remote(xbuf.at[h, e2], xbuf.at[h, e2], ps.at[e2], pr.at[e2], (other, e))

    ppush(0).start()

    def relay(j):
        e2 = lax.rem(e + en - j, en)
        remote(mid, xbuf.at[h, e2], es.at[j], er.at[e2], (c, e2)).wait_recv()
        ppush(j).start()

    loop(en, relay, start=1)
    gcopy.wait()

    def garrive(j):
        c2 = lax.rem(c + cn - j, cn)
        remote(gp, gbuf.at[c2], gs.at[j], gr.at[c2], (c2, e)).wait_recv()

    loop(cn, garrive, start=1)

    def parrive(e2):
        remote(
            xbuf.at[1 - h, e2], xbuf.at[1 - h, e2], ps.at[e2], pr.at[e2], (other, e)
        ).wait_recv()

    loop(en, parrive)
    lanes = 8 * cn
    rows = gbuf[...].reshape(lanes, 128)
    gall[...] = rows

    def group(g):
        spread, same, same_half = slot_gates(cn, rows, g)
        one = jnp.where(same & same_half & (spread > 0.0), 1.0, 0.0).astype(BF16)
        at = pl.multiple_of(g * 2 * cn, 2 * cn)
        for core in range(2):
            xv = xbuf[core, g].astype(F32).reshape(lanes, 128).astype(BF16)
            r = lax.dot_general(
                one, xv, (((0,), (0,)), ((), ())), preferred_element_type=F32
            ).astype(BF16)
            for hf in range(2):
                for k in range(2):
                    lo = hf * 4 * cn + k * 2 * cn
                    f = core * 256 + hf * 128
                    xs[k, pl.ds(at, 2 * cn), f : f + 128] = r[lo : lo + 2 * cn, :]

    loop(en, group)
    for copy in copies:
        copy.wait()
    nchunk = y.shape[0] // 2
    crow = y.shape[1]
    nc = min(256, 2 * half)
    for k in range(2):
        def column(t, k=k):
            at = pl.multiple_of(t * nc, nc)
            r = jnp.dot(xs[k, :, 0:256], wbuf[k, 0, :, pl.ds(at, nc)], preferred_element_type=F32)
            r = r + jnp.dot(
                xs[k, :, 256:512], wbuf[k, 1, :, pl.ds(at, nc)], preferred_element_type=F32
            )
            r = r.astype(BF16)
            for i in range(nchunk):
                y[k * nchunk + i, :, pl.ds(at, nc)] = r[i * crow : (i + 1) * crow, :]

        loop(2 * half // nc, column)
    loop(cn, lambda j: mpush(j).wait_send(), start=1)
    loop(cn, lambda j: gpush(j).wait_send(), start=1)
    loop(en, lambda j: epush(j).wait_send(), start=1)
    loop(en, lambda j: ppush(j).wait_send())


def hidden_kernel(cn, en, y, hid, ybuf, ys, yr, ls):
    c, e = place(cn, en)
    h = lax.rem(c, 2)
    nk = cn // 2
    chip = c // 2
    copy = pltpu.make_async_copy(y.at[chip], ybuf.at[chip], ls.at[0])
    copy.start()
    greet([(1, nk, lambda j: (lax.rem(chip + j, nk) * 2 + h, e))])

    def push(j):
        k = lax.rem(chip + j, nk)
        return remote(y.at[k], ybuf.at[chip], ys.at[j], yr.at[chip], (k * 2 + h, e))

    def arrive(j):
        k = lax.rem(chip + nk - j, nk)
        remote(y.at[k], ybuf.at[k], ys.at[j], yr.at[k], (k * 2 + h, e)).wait_recv()

    loop(nk, lambda j: push(j).start(), start=1)
    copy.wait()
    loop(nk, arrive, start=1)
    half = hid.shape[1]
    rc = 16

    def block(t):
        at = pl.multiple_of(t * rc, rc)
        gate = sum(ybuf[k, pl.ds(at, rc), 0:half].astype(F32) for k in range(nk))
        up = sum(ybuf[k, pl.ds(at, rc), half:].astype(F32) for k in range(nk))
        hid[pl.ds(at, rc), :] = (gate / (1.0 + jnp.exp(-gate)) * up).astype(BF16)

    loop(hid.shape[0] // rc, block)
    loop(nk, lambda j: push(j).wait_send(), start=1)


def down_kernel(cn, en, hid, wd, gall, comb, hbuf, wbuf, obuf, hs, hr, ps, pr, ls):
    c, e = place(cn, en)
    h = lax.rem(c, 2)
    other = c + 1 - 2 * h
    nk = cn // 2
    chip = c // 2
    wcopy = pltpu.make_async_copy(wd, wbuf, ls.at[0])
    hcopy = pltpu.make_async_copy(hid, hbuf.at[h, chip], ls.at[1])
    wcopy.start()
    hcopy.start()
    greet([
        (1, nk, lambda j: (lax.rem(chip + j, nk) * 2 + h, e)),
        (0, 1, lambda j: (other, e)),
    ])

    def push(j):
        k = lax.rem(chip + j, nk)
        return remote(hid, hbuf.at[h, chip], hs.at[j], hr.at[chip], (k * 2 + h, e))

    def ppush(j):
        k = lax.rem(chip + nk - j, nk)
        return remote(hbuf.at[h, k], hbuf.at[h, k], ps.at[k], pr.at[k], (other, e))

    loop(nk, lambda j: push(j).start(), start=1)
    hcopy.wait()
    ppush(0).start()

    def relay(j):
        k = lax.rem(chip + nk - j, nk)
        remote(hid, hbuf.at[h, k], hs.at[j], hr.at[k], (k * 2 + h, e)).wait_recv()
        ppush(j).start()

    loop(nk, relay, start=1)

    def parrive(k):
        remote(
            hbuf.at[1 - h, k], hbuf.at[1 - h, k], ps.at[k], pr.at[k], (other, e)
        ).wait_recv()

    loop(nk, parrive)
    wcopy.wait()
    half = hid.shape[1]
    crow = hid.shape[0]
    each = nk // 2

    def down(k):
        x = k // each
        r = jnp.dot(hbuf[0, k], wbuf[x, 0:half, :], preferred_element_type=F32)
        r = r + jnp.dot(hbuf[1, k], wbuf[x, half:, :], preferred_element_type=F32)
        obuf[x, pl.ds(pl.multiple_of(lax.rem(k, each) * crow, crow), crow), :] = r.astype(BF16)

    loop(nk, down)
    rows = gall[...]
    lanes = 8 * cn
    low = lax.rem(lax.broadcasted_iota(jnp.int32, (lanes, 128), 0), 8) < 4

    def group(g):
        spread, same, same_half = slot_gates(cn, rows, g)
        gates = jnp.where(same, spread, 0.0)[:, : 4 * cn]
        hi = gates.astype(BF16)
        lo = (gates - hi.astype(F32)).astype(BF16)
        at = pl.multiple_of(g * 2 * cn, 2 * cn)
        ov = jnp.concatenate(
            [obuf[0, pl.ds(at, 2 * cn), :], obuf[1, pl.ds(at, 2 * cn), :]], axis=0
        )
        r = jnp.dot(hi, ov, preferred_element_type=F32)
        r = r + jnp.dot(lo, ov, preferred_element_type=F32)
        comb[g] = jnp.where(low, r[:, :128], r[:, 128:]).reshape(cn, 8, 128).astype(BF16)

    loop(en, group)
    loop(nk, lambda j: push(j).wait_send(), start=1)
    loop(nk, lambda j: ppush(j).wait_send())


def return_kernel(cn, en, comb, state, out, r1, r2, es, er, cs, cr, ls):
    c, e = place(cn, en)
    ecopy = pltpu.make_async_copy(comb.at[e], r1.at[e], ls.at[0])
    ecopy.start()
    greet([
        (1, cn, lambda j: (lax.rem(c + j, cn), e)),
        (1, en, lambda j: (c, lax.rem(e + j, en))),
    ])

    def epush(j):
        e2 = lax.rem(e + j, en)
        return remote(comb.at[e2], r1.at[e], es.at[j], er.at[e], (c, e2))

    def earrive(j):
        e2 = lax.rem(e + en - j, en)
        remote(comb.at[e2], r1.at[e2], es.at[j], er.at[e2], (c, e2)).wait_recv()

    loop(en, lambda j: epush(j).start(), start=1)
    ecopy.wait()
    loop(en, earrive, start=1)

    def cpush(j):
        c2 = lax.rem(c + j, cn)
        return remote(r1.at[:, c2], r2.at[c], cs.at[j], cr.at[c], (c2, e))

    def carrive(j):
        c2 = lax.rem(c + cn - j, cn)
        remote(r1.at[:, c2], r2.at[c2], cs.at[j], cr.at[c2], (c2, e)).wait_recv()

    loop(cn, lambda j: cpush(j).start(), start=1)
    ccopy = pltpu.make_async_copy(r1.at[:, c], r2.at[c], ls.at[1])
    ccopy.start()
    ccopy.wait()
    loop(cn, carrive, start=1)
    for i in range(cn):
        s = sum(r2[i, k].astype(F32) for k in range(en))
        for hf in range(2):
            f = i * 256 + hf * 128
            out[:, f : f + 128] = state[:, f : f + 128] + s[4 * hf : 4 * hf + 4, :]
    loop(en, lambda j: epush(j).wait_send(), start=1)
    loop(cn, lambda j: cpush(j).wait_send(), start=1)


def call(body, cn, en, ident, ins, outs, scratch, args):
    return pl.pallas_call(
        functools.partial(body, cn, en),
        out_shape=tuple(jax.ShapeDtypeStruct(s, d) for s, d, _ in outs),
        in_specs=list(ins),
        out_specs=tuple(b for _, _, b in outs),
        scratch_shapes=scratch,
        compiler_params=pltpu.CompilerParams(
            collective_id=ident, has_side_effects=True, vmem_limit_bytes=60 << 20
        ),
        name=body.__name__,
    )(*args)


def gate_blocks(en, expert_ids, gate_values):
    rows = expert_ids.shape[0]
    experts = 2 * en
    hit = expert_ids[:, :, None] == jnp.arange(experts, dtype=jnp.int32)
    dense = jnp.sum(jnp.where(hit, gate_values[:, :, None], 0.0), axis=1)
    named = jnp.any(hit, axis=1).astype(jnp.int32)
    rank = jnp.cumsum(named, axis=0) - named
    ranked = jnp.where(
        rank[:, :, None] == jnp.arange(2, dtype=jnp.int32), dense[:, :, None], 0.0
    )
    blocks = ranked.reshape(rows, en, 4).transpose(1, 0, 2)
    blocks = jnp.concatenate([blocks, blocks], axis=1)
    mine = lax.axis_index("exp")
    spot = jnp.arange(128, dtype=jnp.int32) // 4 == mine
    return jnp.where(spot, jnp.tile(blocks, (1, 1, 32)), 0.0)


def local(cn, en, query, keys, values, out_weight, residual, norm_gain, expert_ids, gate_values,
          w_gate_up, w_down):
    rows, width = query.shape
    d = out_weight.shape[1]
    key_rows = keys.shape[0]
    cols = rows * (width // HD)
    ff = w_down.shape[1]
    half = ff // 2
    fb = w_gate_up.shape[1]
    nk = cn // 2
    slots = 2 * cn * en
    crow = 2 * slots // nk
    gm = gate_blocks(en, expert_ids, gate_values)
    o, st, wother = call(
        attend_kernel, cn, en, 0, [ANY] * 4,
        [((cn, rows, width), BF16, VM), ((cn, 8, 128), F32, VM), ((2, fb, ff), BF16, ANY)],
        [
            pltpu.VMEM((cn, rows, width), BF16),
            pltpu.VMEM((key_rows, HD), BF16),
            pltpu.VMEM((key_rows, HD), BF16),
            pltpu.VMEM((HD, key_rows), BF16),
            pltpu.VMEM((key_rows, cols), F32),
            pltpu.VMEM((8, cols), F32),
            DMA((cn,)), DMA((cn,)), DMA((2,)), DMA((2,)), DMA((3,)),
        ],
        (query, keys, values, w_gate_up),
    )
    p, hm = call(
        project_kernel, cn, en, 1, [ANY] * 3,
        [((en, 8, d // 2), BF16, VM), ((8, 128), F32, VM)],
        [
            pltpu.VMEM((cn, rows, width), BF16),
            pltpu.VMEM((cn, 8, 128), F32),
            pltpu.VMEM((width, d), BF16),
            pltpu.VMEM((128, 128), F32),
            pltpu.VMEM((2 * rows, width), BF16),
            DMA((cn,)), DMA((cn,)), DMA((cn,)), DMA((cn,)), DMA((3,)),
        ],
        (o, st, out_weight),
    )
    state, x, gp = call(
        norm_kernel, cn, en, 2, [ANY, ANY, VM, VM],
        [((4, d), F32, VM), ((cn, 8, 128), BF16, VM), ((8, 128), F32, VM)],
        [
            pltpu.VMEM((en, 8, d // 2), BF16),
            pltpu.VMEM((en, 8, 128), F32),
            DMA((en,)), DMA((en,)), DMA((en,)), DMA((en,)), DMA((2,)),
        ],
        (p, gm, residual, norm_gain.reshape(1, d)),
    )
    y, gall = call(
        expert_kernel, cn, en, 3, [ANY] * 4,
        [((nk, crow, ff), BF16, VM), ((8 * cn, 128), F32, VM)],
        [
            pltpu.VMEM((cn, 8, 128), BF16),
            pltpu.VMEM((cn, 8, 128), F32),
            pltpu.VMEM((2, en, cn, 8, 128), BF16),
            pltpu.VMEM((2, 2, fb, ff), BF16),
            pltpu.VMEM((2, slots, 2 * fb), BF16),
            DMA((cn,)), DMA((cn,)), DMA((cn,)), DMA((cn,)),
            DMA((en,)), DMA((en,)), DMA((en,)), DMA((en,)), DMA((6,)),
        ],
        (x, gp, w_gate_up, wother),
    )
    (hid,) = call(
        hidden_kernel, cn, en, 4, [ANY],
        [((crow, half), BF16, VM)],
        [pltpu.VMEM((nk, crow, ff), BF16), DMA((nk,)), DMA((nk,)), DMA((1,))],
        (y,),
    )
    (comb,) = call(
        down_kernel, cn, en, 5, [ANY, ANY, VM],
        [((en, cn, 8, 128), BF16, VM)],
        [
            pltpu.VMEM((2, nk, crow, half), BF16),
            pltpu.VMEM((2, ff, fb), BF16),
            pltpu.VMEM((2, slots, fb), BF16),
            DMA((nk,)), DMA((nk,)), DMA((nk,)), DMA((nk,)), DMA((2,)),
        ],
        (hid, w_down, gall),
    )
    (layer_out,) = call(
        return_kernel, cn, en, 6, [ANY, VM],
        [((4, d), F32, VM)],
        [
            pltpu.VMEM((en, cn, 8, 128), BF16),
            pltpu.VMEM((cn, en, 8, 128), BF16),
            DMA((en,)), DMA((en,)), DMA((cn,)), DMA((cn,)), DMA((2,)),
        ],
        (comb, state),
    )
    heads = width // HD
    head_max = jnp.max(hm[4:6, : cols // 2].reshape(heads, rows), axis=1)
    return layer_out, head_max


def solution(mesh):
    cn, en = mesh.shape["ctx"], mesh.shape["exp"]
    return jax.shard_map(
        functools.partial(local, cn, en),
        mesh=mesh,
        in_specs=(
            P("ctx", "exp"),
            P("ctx", None),
            P("ctx", None),
            P("exp", None),
            P(("ctx", "exp"), None),
            P(),
            P(("ctx", "exp"), None),
            P(("ctx", "exp"), None),
            P("exp", "ctx", None),
            P("exp", None, "ctx"),
        ),
        out_specs=(P(("ctx", "exp"), None), P("exp")),
        check_vma=False,
    )
```

time: 651 us -> 258 us (0.40)
  the two profiles are of different devices: /device:TPU:225 before, /device:TPU:1 now
where the time goes in v1:
time: 258 us; the launch traced here: 257 us
  Pallas kernels  251 us (97%)
  other arithmetic  3.06 us (1%)
  local copies, waits for them, and re-layouts  2.86 us (1%)
    pallas_call x7, Pallas kernels, call(): pl.pallas_call(functools.partial(body, cn, en), out_shape=tuple((jax.Shap...  251 us

profile of v1, /device:TPU:1, one launch (start us, length us, event | category | flops | bytes accessed | tf_op | source)
XLA Modules:
  0.0 257.4 jit_solution(13178059437957173750)
XLA Ops:
  0.6 0.8 fusion
  1.4 0.1 eq.47
  1.6 0.8 select_reduce_fusion
  2.3 0.1 copy.15
  2.4 0.1 copy.14
  2.6 0.1 select_bitcast_fusion
  2.6 0.1 pad_maximum_fusion
  2.7 0.1 copy.16
  2.8 0.1 tile.4
  2.9 0.2 copy.17
  3.1 0.7 broadcast_select_fusion.gm
  3.7 32.2 %attend_kernel.1 = (bf16[16,64,512]{2,1,0:T(8,128)(2,1)}, f32[16,8,128]{2,1,0:T(8,128)}, bf16[2,256,1536]{2,1,0:T(8,128)(2,1)}) custom-call(bf16[64,512]{1,0:T(8,128)(2,1)} %q.1, bf16[2048,512]{1,0:T(8,128)(2,1)} %keys.1, bf16[2048,512]{1,0:T(8,128)(2,1)} %vals.1, bf16[2,256,3072]{2,1,0:T(8,128)(2,1)} %w.5), custom_call_target="tpu_custom_call" | custom-call | tf_op jit(solution)/shard_map/attend_kernel/pallas_call | solution.py:582
  35.9 26.1 %project_kernel.1 = (bf16[16,8,2048]{2,1,0:T(8,128)(2,1)}, f32[8,128]{1,0:T(8,128)}) custom-call(bf16[16,64,512]{2,1,0:T(8,128)(2,1)} %get-tuple-element.12.o, f32[16,8,128]{2,1,0:T(8,128)} %get-tuple-element.13.st, bf16[512,4096]{1,0:T(8,128)(2,1)} %w.4), custom_call_target="tpu_custom_call" | custom-call | tf_op jit(solution)/shard_map/project_kernel/pallas_call | solution.py:582
  62.0 24.4 %norm_kernel.1 = (f32[4,4096]{1,0:T(4,128)}, bf16[16,8,128]{2,1,0:T(8,128)(2,1)}, f32[8,128]{1,0:T(8,128)}) custom-call(bf16[16,8,2048]{2,1,0:T(8,128)(2,1)} %get-tuple-element.14.p, f32[16,8,128]{2,1,0:T(8,128)} %broadcast_select_fusion.gm, bf16[4,4096]{1,0:T(4,128)(2,1)} %residual.1, f32[1,4096]{1,0:T(1,128)} %bitcast.9), custom_call_target="tpu_custom_call" | custom-call | tf_op jit(solution)/shard_map/norm_kernel/pallas_call | solution.py:582
  86.4 0.7 slice.3
  87.1 0.1 reshape.35
  87.1 0.6 reduce_max.9
  87.8 43.5 %expert_kernel.1 = (bf16[8,128,1536]{2,1,0:T(8,128)(2,1)}, f32[128,128]{1,0:T(8,128)}) custom-call(bf16[16,8,128]{2,1,0:T(8,128)(2,1)} %get-tuple-element.15.x, f32[8,128]{1,0:T(8,128)} %get-tuple-element.16.gp, bf16[2,256,3072]{2,1,0:T(8,128)(2,1)} %w.5, bf16[2,256,1536]{2,1,0:T(8,128)(2,1)} %get-tuple-element.17.wother), custom_call_target="tpu_custom_call" | custom-call | tf_op jit(solution)/shard_map/expert_kernel/pallas_call | solution.py:582
  131.3 50.5 %hidden_kernel.1.hid = bf16[128,768]{1,0:T(8,128)(2,1)} custom-call(bf16[8,128,1536]{2,1,0:T(8,128)(2,1)} %get-tuple-element.18.y), custom_call_target="tpu_custom_call" | custom-call | tf_op jit(solution)/shard_map/hidden_kernel/pallas_call | solution.py:582
  181.8 40.3 %down_kernel.1.comb = bf16[16,16,8,128]{3,2,1,0:T(8,128)(2,1)} custom-call(bf16[128,768]{1,0:T(8,128)(2,1)} %hidden_kernel.1.hid, bf16[2,1536,256]{2,1,0:T(8,128)(2,1)} %wd.1, f32[128,128]{1,0:T(8,128)} %get-tuple-element.19.gall), custom_call_target="tpu_custom_call" | custom-call | tf_op jit(solution)/shard_map/down_kernel/pallas_call | solution.py:582
  222.1 33.8 %return_kernel.1 = f32[4,4096]{1,0:T(4,128)} custom-call(bf16[16,16,8,128]{3,2,1,0:T(8,128)(2,1)} %down_kernel.1.comb, f32[4,4096]{1,0:T(4,128)} %get-tuple-element.20.state), custom_call_target="tpu_custom_call" | custom-call | tf_op jit(solution)/shard_map/return_kernel/pallas_call | solution.py:582
  255.9 1.5 copy.19
  (7 shorter events, 0.1 us)

commit v2 on v0

v2 whole, which is shorter than its diff:
```python
import functools
import math

import jax
import jax.numpy as jnp
from jax import lax
from jax.experimental import pallas as pl
from jax.experimental.pallas import tpu as pltpu
from jax.sharding import PartitionSpec as P

HEADS = 64
KVH = 4
HD = 128
EPS = 1e-06
NEG = -1e30
MESH = pl.DeviceIdType.MESH
ANY = pl.BlockSpec(memory_space=pl.ANY)
VM = pl.BlockSpec(memory_space=pltpu.VMEM)
F32 = jnp.float32
BF16 = jnp.bfloat16
DMA = pltpu.SemaphoreType.DMA


def loop(n, body, start=0):
    def step(i, carry):
        body(i)
        return carry

    lax.fori_loop(start, n, step, 0)


def place(cn, en):
    return lax.axis_index("ctx"), lax.axis_index("exp")


def greet(targets):
    barrier = pltpu.get_barrier_semaphore()
    total = 0
    for first, last, device in targets:
        loop(
            last,
            lambda j, device=device: pl.semaphore_signal(
                barrier, inc=1, device_id=device(j), device_id_type=MESH
            ),
            start=first,
        )
        total += last - first
    pl.semaphore_wait(barrier, total)


def remote(src, dst, send, recv, device):
    return pltpu.make_async_remote_copy(
        src_ref=src,
        dst_ref=dst,
        send_sem=send,
        recv_sem=recv,
        device_id=device,
        device_id_type=MESH,
    )


def slot_gates(cn, gall, group):
    lanes = 8 * cn
    row = lax.broadcasted_iota(jnp.int32, (lanes, lanes), 0)
    col = lax.broadcasted_iota(jnp.int32, (lanes, lanes), 1)
    k = lax.broadcasted_iota(jnp.int32, (128, lanes), 0)
    which = lax.rem(lax.broadcasted_iota(jnp.int32, (128, lanes), 1) // cn, 4)
    pick = (k == 4 * group + which).astype(F32)
    spread = jnp.dot(gall, pick, preferred_element_type=F32, precision=lax.Precision.HIGHEST)
    same = row // 8 == lax.rem(col, cn)
    same_half = lax.rem(row // 4, 2) == col // (4 * cn)
    return spread, same, same_half


def layer_kernel(cn, en, q, keys, vals, w, outw, wd, ids, gates, residual, gain, out, hm,
                 qbuf, kbuf, vbuf, vt, sbuf, mbuf, osend, obuf, stsend, stbuf, hmsend, hmbuf,
                 gsend, gbuf, gpsend, gall, owbuf, coef, a2, psend, pbuf, state, xsend, mid, xbuf,
                 wbuf, slotm, gatem, xs, ysend, ybuf, hbuf, wdbuf, csend, r1, r2,
                 qs, qr, os_, or_, ss, sr, ms, mr, gs, gr, gps, gpr, ws, wr, ps, pr, xsm, xrm,
                 es, er, es2, er2, ys, yr, hs, hr, hs2, hr2, cs_, cr_, rs_, rr_, ls):
    c, e = place(cn, en)
    h = lax.rem(c, 2)
    other = c + 1 - 2 * h
    chip = c // 2
    nk = cn // 2
    gq = cn // 4
    nq = en // gq
    rows, width = q.shape
    heads = width // HD
    key_rows = keys.shape[0]
    half = w.shape[2] // 4
    cols = heads * rows
    hc = cols // 2
    lanes = 8 * cn
    d = outw.shape[1]
    n = d // 2

    def ctx(j):
        return (lax.rem(c + j, cn), e)

    def exp(j):
        return (c, lax.rem(e + j, en))

    def csrc(j):
        return lax.rem(c + cn - j, cn)

    def esrc(j):
        return lax.rem(e + en - j, en)

    kv = pl.multiple_of((e * heads // (HEADS // KVH)) * HD, HD)
    kcopy = pltpu.make_async_copy(keys.at[:, pl.ds(kv, HD)], kbuf, ls.at[0])
    vcopy = pltpu.make_async_copy(vals.at[:, pl.ds(kv, HD)], vbuf, ls.at[1])
    qcopy = pltpu.make_async_copy(q, qbuf.at[c], ls.at[2])
    owcopy = pltpu.make_async_copy(outw, owbuf, ls.at[3])
    wdcopy = pltpu.make_async_copy(wd, wdbuf, ls.at[4])
    wcopies = [
        pltpu.make_async_copy(
            w.at[:, :, pl.ds(pl.multiple_of(part * 2 * half + h * half, 128), half)],
            wbuf.at[:, h, :, pl.ds(part * half, half)],
            ls.at[5 + part],
        )
        for part in range(2)
    ]
    for copy in [kcopy, vcopy, qcopy]:
        copy.start()

    spot = lax.broadcasted_iota(jnp.int32, (4, 128), 1)
    dense = jnp.zeros((4, 128), F32)
    for k in range(ids.shape[1]):
        dense = dense + jnp.where(ids[:, k : k + 1] == spot // 2, gates[:, k : k + 1], 0.0)
    named = (dense > 0.0).astype(jnp.int32)
    r0 = named[0:1, :]
    r1_ = r0 + named[1:2, :]
    r2_ = r1_ + named[2:3, :]
    rank = jnp.concatenate([jnp.zeros((1, 128), jnp.int32), r0, r1_, r2_], axis=0)
    table = jnp.where(rank == lax.rem(spot, 2), dense, 0.0)
    gsend[...] = jnp.concatenate([table, table], axis=0)
    gbuf[e] = gsend[...]

    greet([(1, cn, ctx), (1, en, exp)])

    def qpush(j):
        return remote(q, qbuf.at[c], qs.at[j], qr.at[c], ctx(j))

    loop(cn, lambda j: qpush(j).start(), start=1)

    def gpush(j):
        return remote(gsend, gbuf.at[e], gs.at[j], gr.at[e], exp(j))

    loop(en, lambda j: gpush(j).start(), start=1)

    def wpush(part):
        off = pl.multiple_of(part * 2 * half + (1 - h) * half, 128)
        return remote(
            w.at[:, :, pl.ds(off, half)],
            wbuf.at[:, h, :, pl.ds(part * half, half)],
            ws.at[part],
            wr.at[part],
            (other, e),
        )

    wpush(0).start()
    wpush(1).start()
    kcopy.wait()
    vcopy.wait()
    qcopy.wait()
    for copy in wcopies + [owcopy, wdcopy]:
        copy.start()
    vt[...] = vbuf[...].astype(F32).T.astype(BF16)
    mbuf[...] = jnp.full(mbuf.shape, NEG, F32)
    scale = 1.0 / math.sqrt(HD)
    scale2 = scale * math.log2(math.e)
    first_q = key_rows * cn - rows * cn
    kc = min(512, key_rows)

    def opush(j):
        cs = csrc(j)
        return remote(osend.at[cs], obuf.at[c], os_.at[j], or_.at[c], (cs, e))

    def spush(j):
        cs = csrc(j)
        return remote(stsend.at[cs], stbuf.at[c], ss.at[j], sr.at[c], (cs, e))

    def osend_start(j):
        spush(j).start()
        opush(j).start()

    def attend(j):
        cs = csrc(j)

        @pl.when(j > 0)
        def _():
            remote(q, qbuf.at[cs], qs.at[0], qr.at[cs], (cs, e)).wait_recv()

        @pl.when(j > 1)
        def _():
            osend_start(j - 1)

        qv = qbuf[cs]
        qcat = jnp.concatenate([qv[:, i * HD : (i + 1) * HD] for i in range(heads)], axis=0)
        for t in range(key_rows // kc):
            sbuf[t * kc : (t + 1) * kc, :] = lax.dot_general(
                kbuf[t * kc : (t + 1) * kc, :],
                qcat,
                (((1,), (1,)), ((), ())),
                preferred_element_type=F32,
            )

        @pl.when(c == cn - 1)
        def _():
            lane = lax.rem(lax.broadcasted_iota(jnp.int32, (1, cols), 1), rows)
            limit = first_q + cs * rows + lane - c * key_rows
            for t in range(key_rows // kc):
                kpos = t * kc + lax.broadcasted_iota(jnp.int32, (kc, cols), 0)
                sbuf[t * kc : (t + 1) * kc, :] = jnp.where(
                    kpos <= limit, sbuf[t * kc : (t + 1) * kc, :], NEG
                )

        m = jnp.max(sbuf[0:kc, :], axis=0, keepdims=True)
        for t in range(1, key_rows // kc):
            m = jnp.maximum(m, jnp.max(sbuf[t * kc : (t + 1) * kc, :], axis=0, keepdims=True))
        total = jnp.zeros((1, cols), F32)
        acc = jnp.zeros((HD, cols), F32)
        for t in range(key_rows // kc):
            p = jnp.exp2((sbuf[t * kc : (t + 1) * kc, :] - m) * scale2)
            total = total + jnp.sum(p, axis=0, keepdims=True)
            acc = acc + jnp.dot(
                vt[:, t * kc : (t + 1) * kc], p.astype(BF16), preferred_element_type=F32
            )
        got = acc.T.astype(BF16)
        for i in range(heads):
            osend[cs, :, i * HD : (i + 1) * HD] = got[i * rows : (i + 1) * rows, :]
        msc = m * scale
        stsend[cs, 0:1, :hc] = msc[:, :hc]
        stsend[cs, 1:2, :hc] = msc[:, hc:]
        stsend[cs, 2:3, :hc] = total[:, :hc]
        stsend[cs, 3:4, :hc] = total[:, hc:]
        mbuf[0:1, :] = jnp.maximum(mbuf[0:1, :], msc)

    loop(cn, attend)
    hmsend[0:1, :hc] = mbuf[0:1, :hc]
    hmsend[1:2, :hc] = mbuf[0:1, hc:]

    def garrive(j):
        e2 = esrc(j)
        remote(gsend, gbuf.at[e2], gs.at[j], gr.at[e2], (c, e2)).wait_recv()

    loop(en, garrive, start=1)
    osend_start(cn - 1)
    gr_ = lax.broadcasted_iota(jnp.int32, (128, 128), 0)
    gc_ = lax.broadcasted_iota(jnp.int32, (128, 128), 1)
    pick = (gr_ == 4 * e + lax.rem(gc_, 4)).astype(F32)
    picked = jnp.dot(
        gbuf[...].reshape(8 * en, 128), pick, preferred_element_type=F32,
        precision=lax.Precision.HIGHEST,
    )
    picked = jnp.where(gr_[: 8 * en] // 8 == gc_[: 8 * en] // 4, picked, 0.0)
    gpsend[...] = jnp.sum(picked.reshape(en, 8, 128), axis=0)
    gall[c] = gpsend[...]
    obuf[c] = osend[c]
    stbuf[c] = stsend[c]
    hmbuf[c] = hmsend[...]

    def sarrive(j):
        c2 = csrc(j)
        remote(stsend.at[c2], stbuf.at[c2], ss.at[j], sr.at[c2], (c2, e)).wait_recv()

    def oarrive(j):
        c2 = csrc(j)
        remote(osend.at[c2], obuf.at[c2], os_.at[j], or_.at[c2], (c2, e)).wait_recv()

    loop(cn, sarrive, start=1)
    peak = functools.reduce(jnp.maximum, [stbuf[i, 0:2, :] for i in range(cn)])
    weights = [jnp.exp(stbuf[i, 0:2, :] - peak) for i in range(cn)]
    total = sum(wt * stbuf[i, 2:4, :] for i, wt in enumerate(weights))
    coef[...] = jnp.zeros(coef.shape, F32)
    for i in range(cn):
        coef[2 * i : 2 * i + 2, :] = weights[i] / total
    turned = coef[...].T
    dup = (
        lax.broadcasted_iota(jnp.int32, (2 * rows, rows), 1)
        == lax.broadcasted_iota(jnp.int32, (2 * rows, rows), 0) // 8 * 4
        + lax.rem(lax.broadcasted_iota(jnp.int32, (2 * rows, rows), 0), 4)
    ).astype(BF16)
    loop(cn, oarrive, start=1)
    for i in range(heads):
        lo = (i % (heads // 2)) * rows
        acc = jnp.zeros((rows, HD), F32)
        for k in range(cn):
            at = 2 * k + i // (heads // 2)
            acc = acc + turned[lo : lo + rows, at : at + 1] * obuf[
                k, :, i * HD : (i + 1) * HD
            ].astype(F32)
        a2[:, i * HD : (i + 1) * HD] = jnp.dot(
            dup, acc.astype(BF16), preferred_element_type=F32
        ).astype(BF16)
    owcopy.wait()
    left = a2[...]
    nc = min(256, n)
    low = lax.rem(lax.broadcasted_iota(jnp.int32, (2 * rows, nc), 0), 8) < 4

    def column(t):
        at = pl.multiple_of(t * nc, nc)
        v0 = jnp.dot(left, owbuf[:, pl.ds(at, nc)], preferred_element_type=F32)
        v1 = jnp.dot(left, owbuf[:, pl.ds(at + n, nc)], preferred_element_type=F32)
        v = jnp.where(low, v0, v1)
        for k in range(en):
            psend[k, :, pl.ds(at, nc)] = v[8 * k : 8 * k + 8, :].astype(BF16)

    loop(n // nc, column)

    def ppush(j):
        e2 = lax.rem(e + j, en)
        return remote(psend.at[e2], pbuf.at[e], ps.at[j], pr.at[e], (c, e2))

    def parrive(j):
        e2 = esrc(j)
        remote(psend.at[e2], pbuf.at[e2], ps.at[j], pr.at[e2], (c, e2)).wait_recv()

    loop(en, lambda j: ppush(j).start(), start=1)

    def gppush(j):
        return remote(gpsend, gall.at[c], gps.at[j], gpr.at[c], ctx(j))

    def gparrive(j):
        c2 = csrc(j)
        remote(gpsend, gall.at[c2], gps.at[j], gpr.at[c2], (c2, e)).wait_recv()

    def hmpush(j):
        return remote(hmsend, hmbuf.at[c], ms.at[j], mr.at[c], ctx(j))

    def hmarrive(j):
        c2 = csrc(j)
        remote(hmsend, hmbuf.at[c2], ms.at[j], mr.at[c2], (c2, e)).wait_recv()

    loop(cn, lambda j: gppush(j).start(), start=1)
    loop(cn, lambda j: hmpush(j).start(), start=1)
    pbuf[e] = psend[e]
    loop(cn, gparrive, start=1)
    rows_all = gall[...].reshape(lanes, 128)

    def tables(g):
        spread, same, same_half = slot_gates(cn, rows_all, g)
        slotm[g] = jnp.where(same & same_half & (spread > 0.0), 1.0, 0.0).T.astype(BF16)
        part = jnp.where(same, spread, 0.0)
        hi = part.astype(BF16).astype(F32)
        first = lax.broadcasted_iota(jnp.int32, (lanes, lanes), 1) < lanes // 2
        gatem[g] = jnp.where(first, hi, part - hi).astype(BF16)

    loop(en, tables)
    loop(en, parrive, start=1)
    s = sum(pbuf[i].astype(F32) for i in range(en))
    s0 = s[0:4, :] + residual[:, :n].astype(F32)
    s1 = s[4:8, :] + residual[:, n:].astype(F32)
    state[:, :n] = s0
    state[:, n:] = s1
    mean = (
        jnp.sum(s0 * s0, axis=1, keepdims=True) + jnp.sum(s1 * s1, axis=1, keepdims=True)
    ) * (1.0 / d)
    inv = lax.rsqrt(mean + EPS)
    n0 = s0 * inv * gain[:, :n]
    n1 = s1 * inv * gain[:, n:]
    for i in range(cn):
        part, off = (n0, i * 256) if i * 256 < n else (n1, i * 256 - n)
        xsend[i] = jnp.concatenate(
            [part[:, off : off + 128], part[:, off + 128 : off + 256]], axis=0
        ).astype(BF16)

    def xpush(j):
        c2 = lax.rem(c + j, cn)
        return remote(xsend.at[c2], mid.at[c], xsm.at[j], xrm.at[c], (c2, e))

    def xarrive(j):
        c2 = csrc(j)
        remote(xsend.at[c2], mid.at[c2], xsm.at[j], xrm.at[c2], (c2, e)).wait_recv()

    loop(cn, lambda j: xpush(j).start(), start=1)
    mid[c] = xsend[c]
    loop(cn, xarrive, start=1)

    def epush(j):
        return remote(mid, xbuf.at[h, e], es.at[j], er.at[e], exp(j))

    def erelay(j):
        e2 = esrc(j)
        return remote(xbuf.at[h, e2], xbuf.at[h, e2], es2.at[e2], er2.at[e2], (other, e))

    loop(en, lambda j: epush(j).start(), start=1)
    own = remote(mid, xbuf.at[h, e], es2.at[e], er2.at[e], (other, e))
    own.start()
    xbuf[h, e] = mid[...]

    def forward(j):
        e2 = esrc(j)
        remote(mid, xbuf.at[h, e2], es.at[j], er.at[e2], (c, e2)).wait_recv()
        erelay(j).start()

    loop(en, forward, start=1)
    for copy in wcopies:
        copy.wait()
    wpush(0).wait()
    wpush(1).wait()
    sc = 2 * cn
    yc = min(512, 2 * half)

    def ypush(qi, j):
        k = lax.rem(chip + j, nk)
        return remote(
            ysend.at[qi, k], ybuf.at[chip, qi], ys.at[qi, j], yr.at[chip, qi], (k * 2 + h, e)
        )

    def expert_in(qi):
        def group(gl):
            g = qi * gq + gl
            remote(
                xbuf.at[1 - h, g], xbuf.at[1 - h, g], es2.at[g], er2.at[g], (other, e)
            ).wait_recv()
            at = pl.multiple_of(gl * sc, sc)
            for core in range(2):
                xv = xbuf[core, g].astype(F32).reshape(lanes, 128).astype(BF16)
                r = jnp.dot(slotm[g], xv, preferred_element_type=F32).astype(BF16)
                for hf in range(2):
                    for k in range(2):
                        lo = hf * 2 * sc + k * sc
                        f = core * 256 + hf * 128
                        xs[k, pl.ds(at, sc), f : f + 128] = r[lo : lo + sc, :]

        loop(gq, group)
        for x in range(2):
            def ycol(t, x=x):
                at = pl.multiple_of(t * yc, yc)
                r = jnp.dot(
                    xs[x, :, 0:256], wbuf[x, 0, :, pl.ds(at, yc)], preferred_element_type=F32
                )
                r = r + jnp.dot(
                    xs[x, :, 256:512], wbuf[x, 1, :, pl.ds(at, yc)], preferred_element_type=F32
                )
                r = r.astype(BF16)
                for k in range(nk):
                    ysend[qi, k, x, :, pl.ds(at, yc)] = r[k * cn : (k + 1) * cn, :]

            loop(2 * half // yc, ycol)
        loop(nk, lambda j: ypush(qi, j).start(), start=1)

    loop(nq, expert_in)

    def hpush(qi, j):
        k = lax.rem(chip + j, nk)
        slot = hbuf.at[h, chip, qi]
        return remote(slot, slot, hs.at[qi, j], hr.at[chip, qi], (k * 2 + h, e))

    def hrelay(qi, k):
        slot = hbuf.at[h, k, qi]
        return remote(slot, slot, hs2.at[qi, k], hr2.at[k, qi], (other, e))

    def reduce_in(qi):
        def yarrive(j):
            k = lax.rem(chip + nk - j, nk)
            remote(
                ysend.at[qi, k], ybuf.at[k, qi], ys.at[qi, j], yr.at[k, qi], (k * 2 + h, e)
            ).wait_recv()

        ybuf[chip, qi] = ysend[qi, chip]
        loop(nk, yarrive, start=1)
        for x in range(2):
            up = sum(ybuf[k, qi, x, :, half:].astype(F32) for k in range(nk))
            gate = sum(ybuf[k, qi, x, :, 0:half].astype(F32) for k in range(nk))
            hbuf[h, chip, qi, x] = (gate / (1.0 + jnp.exp(-gate)) * up).astype(BF16)
        loop(nk, lambda j: hpush(qi, j).start(), start=1)
        hrelay(qi, chip).start()

    def relay(qi):
        def one(j):
            k = lax.rem(chip + nk - j, nk)
            slot = hbuf.at[h, k, qi]
            remote(slot, slot, hs.at[qi, j], hr.at[k, qi], (k * 2 + h, e)).wait_recv()
            hrelay(qi, k).start()

        loop(nk, one, start=1)

    low128 = lax.rem(lax.broadcasted_iota(jnp.int32, (lanes, 128), 0), 8) < 4

    def cpush(e2):
        return remote(csend.at[e2], r1.at[e], cs_.at[e2], cr_.at[e], (c, e2))

    def expert_out(qi):
        def harrive(k):
            slot = hbuf.at[1 - h, k, qi]
            remote(slot, slot, hs2.at[qi, k], hr2.at[k, qi], (other, e)).wait_recv()

        loop(nk, harrive)
        outs = []
        for x in range(2):
            r = jnp.zeros((nk * cn, 256), F32)
            for hh in range(2):
                left = hbuf[hh, :, qi, x].reshape(nk * cn, half)
                r = r + jnp.dot(
                    left, wdbuf[x, hh * half : (hh + 1) * half, :], preferred_element_type=F32
                )
            outs.append(r.astype(BF16))
        for gl in range(gq):
            g = qi * gq + gl
            ov = [o[gl * sc : (gl + 1) * sc, :] for o in outs]
            ov = jnp.concatenate(ov + ov, axis=0)
            r = jnp.dot(gatem[g], ov, preferred_element_type=F32)
            csend[g] = jnp.where(low128, r[:, :128], r[:, 128:]).reshape(cn, 8, 128).astype(BF16)
        for gl in range(gq):
            g = qi * gq + gl

            @pl.when(g != e)
            def _():
                cpush(g).start()

    wdcopy.wait()
    reduce_in(0)
    for qi in range(1, nq):
        reduce_in(qi)
        relay(qi - 1)
        if qi > 1:
            expert_out(qi - 2)
    relay(nq - 1)
    expert_out(nq - 2)
    expert_out(nq - 1)
    r1[e] = csend[e]

    def carrive(j):
        e2 = esrc(j)
        remote(csend.at[e2], r1.at[e2], cs_.at[e2], cr_.at[e2], (c, e2)).wait_recv()

    loop(cn, hmarrive, start=1)
    top = functools.reduce(jnp.maximum, [hmbuf[i] for i in range(cn)])
    place4 = lax.broadcasted_iota(jnp.int32, (1, heads), 1)
    best = jnp.zeros((1, heads), F32)
    for i in range(heads):
        a, b = i // (heads // 2), i % (heads // 2)
        peak1 = jnp.max(top[a : a + 1, b * rows : (b + 1) * rows], axis=1, keepdims=True)
        best = jnp.where(place4 == i, peak1, best)
    hm[...] = best
    loop(en, carrive, start=1)

    def rpush(j):
        c2 = lax.rem(c + j, cn)
        return remote(r1.at[:, c2], r2.at[c], rs_.at[j], rr_.at[c], (c2, e))

    def rarrive(j):
        c2 = csrc(j)
        remote(r1.at[:, c2], r2.at[c2], rs_.at[j], rr_.at[c2], (c2, e)).wait_recv()

    loop(cn, lambda j: rpush(j).start(), start=1)
    r2[c] = r1[:, c]
    loop(cn, rarrive, start=1)
    for i in range(cn):
        s = sum(r2[i, k].astype(F32) for k in range(en))
        for hf in range(2):
            f = i * 256 + hf * 128
            out[:, f : f + 128] = state[:, f : f + 128] + s[4 * hf : 4 * hf + 4, :]

    for push in (qpush, opush, spush, gppush, hmpush, xpush, rpush):
        loop(cn, lambda j, push=push: push(j).wait_send(), start=1)
    for push in (gpush, ppush, epush, erelay):
        loop(en, lambda j, push=push: push(j).wait_send(), start=1)
    own.wait_send()
    loop(en, lambda j: cpush(lax.rem(e + j, en)).wait_send(), start=1)
    for qi in range(nq):
        loop(nk, lambda j, qi=qi: ypush(qi, j).wait_send(), start=1)
        loop(nk, lambda j, qi=qi: hpush(qi, j).wait_send(), start=1)
        loop(nk, lambda k, qi=qi: hrelay(qi, k).wait_send())


def local(cn, en, query, keys, values, out_weight, residual, norm_gain, expert_ids, gate_values,
          w_gate_up, w_down):
    rows, width = query.shape
    heads = width // HD
    d = out_weight.shape[1]
    key_rows = keys.shape[0]
    cols = rows * heads
    ff = w_down.shape[1]
    half = ff // 2
    fb = w_gate_up.shape[1]
    nk = cn // 2
    gq = cn // 4
    nq = en // gq
    v = pltpu.VMEM
    layer_out, head_max = pl.pallas_call(
        functools.partial(layer_kernel, cn, en),
        out_shape=(
            jax.ShapeDtypeStruct((4, d), F32),
            jax.ShapeDtypeStruct((1, heads), F32),
        ),
        in_specs=[ANY] * 6 + [VM] * 4,
        out_specs=(VM, VM),
        scratch_shapes=[
            v((cn, rows, width), BF16),
            v((key_rows, HD), BF16),
            v((key_rows, HD), BF16),
            v((HD, key_rows), BF16),
            v((key_rows, cols), F32),
            v((8, cols), F32),
            v((cn, rows, width), BF16),
            v((cn, rows, width), BF16),
            v((cn, 8, 128), F32),
            v((cn, 8, 128), F32),
            v((8, 128), F32),
            v((cn, 8, 128), F32),
            v((8, 128), F32),
            v((en, 8, 128), F32),
            v((8, 128), F32),
            v((cn, 8, 128), F32),
            v((width, d), BF16),
            v((128, 128), F32),
            v((2 * rows, width), BF16),
            v((en, 8, d // 2), BF16),
            v((en, 8, d // 2), BF16),
            v((4, d), F32),
            v((cn, 8, 128), BF16),
            v((cn, 8, 128), BF16),
            v((2, en, cn, 8, 128), BF16),
            v((2, 2, fb, ff), BF16),
            v((en, 8 * cn, 8 * cn), BF16),
            v((en, 8 * cn, 8 * cn), BF16),
            v((2, gq * 2 * cn, 2 * fb), BF16),
            v((nq, nk, 2, cn, ff), BF16),
            v((nk, nq, 2, cn, ff), BF16),
            v((2, nk, nq, 2, cn, half), BF16),
            v((2, ff, fb), BF16),
            v((en, cn, 8, 128), BF16),
            v((en, cn, 8, 128), BF16),
            v((cn, en, 8, 128), BF16),
            DMA((cn,)), DMA((cn,)), DMA((cn,)), DMA((cn,)), DMA((cn,)), DMA((cn,)),
            DMA((cn,)), DMA((cn,)), DMA((en,)), DMA((en,)), DMA((cn,)), DMA((cn,)),
            DMA((2,)), DMA((2,)), DMA((en,)), DMA((en,)), DMA((cn,)), DMA((cn,)),
            DMA((en,)), DMA((en,)), DMA((en,)), DMA((en,)),
            DMA((nq, nk)), DMA((nk, nq)), DMA((nq, nk)), DMA((nk, nq)),
            DMA((nq, nk)), DMA((nk, nq)),
            DMA((en,)), DMA((en,)), DMA((cn,)), DMA((cn,)), DMA((7,)),
        ],
        compiler_params=pltpu.CompilerParams(
            collective_id=0, has_side_effects=True, vmem_limit_bytes=60 << 20
        ),
        name="layer_kernel",
    )(
        query, keys, values, w_gate_up, out_weight, w_down, expert_ids, gate_values, residual,
        norm_gain.reshape(1, d),
    )
    return layer_out, head_max.reshape(heads)


def solution(mesh):
    cn, en = mesh.shape["ctx"], mesh.shape["exp"]
    return jax.shard_map(
        functools.partial(local, cn, en),
        mesh=mesh,
        in_specs=(
            P("ctx", "exp"),
            P("ctx", None),
            P("ctx", None),
            P("exp", None),
            P(("ctx", "exp"), None),
            P(),
            P(("ctx", "exp"), None),
            P(("ctx", "exp"), None),
            P("exp", "ctx", None),
            P("exp", None, "ctx"),
        ),
        out_specs=(P(("ctx", "exp"), None), P("exp")),
        check_vma=False,
    )
```

time: 651 us -> 175 us (0.27)
  waiting for transfers between devices: 405 us -> 0 us
  Pallas kernels: 0 us -> 171 us
  blocking collectives: 102 us -> 0 us
  matrix products: 52 us -> 0 us
  local copies, waits for them, and re-layouts: 41.2 us -> 2.59 us
  other arithmetic: 22.8 us -> 0 us
  between operations: 14.6 us -> 0.64 us
  starting transfers between devices: 6.74 us -> 0 us
    pallas_call x0 -> x1, Pallas kernels: none -> 171 us  [local(): pl.pallas_call(functools.partial(layer_kernel, cn, en), out_shape=(jax.Sh...]
    psum x1 -> x0, waiting for transfers between devices: 161 us -> none  [local(): lax.psum(jnp.einsum('mxd,xdf->mxf', part_rows, w_gate_up, preferred_eleme...]
    unnamed x5 -> x0, waiting for transfers between devices: 123 us -> none
    all_gather x2 -> x0, waiting for transfers between devices: 121 us -> none  [the longest x1 77 us: local(): lax.all_gather(k_head, 'ctx', axis=0, tiled=True)]
    all_to_all x3 -> x0, blocking collectives: 67.1 us -> none  [the longest x1 29.1 us: local(): lax.all_to_all(outgoing, 'ctx', split_axis=4, concat_axis=1, tiled=True)]
    dot_general x7 -> x0, matrix products: 52 us -> none  [the longest x1 19.1 us: attend_block(): jnp.einsum('rd,kd->rk', q_rows, k_block, preferred_element_type=jnp.float32)]
    pmax x1 -> x0, blocking collectives: 35.4 us -> none  [local(): head_max = lax.pmax(head_peak, 'ctx')]
    reduce_sum x3 -> x0, other arithmetic: 16.4 us -> none  [the longest x1 15.1 us: attend_block(): row_total = jnp.sum(weights, axis=1)]
  transfers between devices with their start and end apart: 5 -> 0, of which waited for: 4 -> 0; matrix products, arithmetic and copies ran while one was open for 6% -> 0% of each run, Pallas kernels for 0% -> 0%
where the time goes in v2:
time: 175 us
  Pallas kernels  171 us (98%)
  local copies, waits for them, and re-layouts  2.59 us (1%)
    pallas_call x1, Pallas kernels, local(): pl.pallas_call(functools.partial(layer_kernel, cn, en), out_shape=(jax.Sh...  171 us

profile of v2, /device:TPU:225, one launch (start us, length us, event | category | flops | bytes accessed | tf_op | source)
XLA Modules:
  0.0 174.6 jit_solution(12189485261599367058)
XLA Ops:
  0.6 171.4 %layer_kernel.1 = (f32[4,4096]{1,0:T(4,128)}, f32[1,4]{1,0:T(1,128)}) custom-call(bf16[64,512]{1,0:T(8,128)(2,1)} %q.1, bf16[2048,512]{1,0:T(8,128)(2,1)} %keys.1, bf16[2048,512]{1,0:T(8,128)(2,1)} %vals.1, bf16[2,256,3072]{2,1,0:T(8,128)(2,1)} %w.1, bf16[512,4096]{1,0:T(8,128)(2,1)} %outw.1, bf16[2,1536,256]{2,1,0:T(8,128)(2,1)} %wd.1, s32[4,8]{1,0:T(4,128)} %ids.1, ...), custom_call_target="tpu_custom_call" | custom-call | tf_op jit(solution)/shard_map/layer_kernel/pallas_call | solution.py:584
  172.0 1.5 copy.14
  173.5 1.1 copy.15

commit v3 on v2

--- a/solution.py
+++ b/solution.py
@@ -139,10 +139,21 @@
 
     greet([(1, cn, ctx), (1, en, exp)])
 
-    def qpush(j):
-        return remote(q, qbuf.at[c], qs.at[j], qr.at[c], ctx(j))
-
-    loop(cn, lambda j: qpush(j).start(), start=1)
+    def asrc(j):
+        k = lax.rem(chip + nk - j // 2, nk)
+        return 2 * k + jnp.where(lax.rem(j, 2) == 0, h, 1 - h)
+
+    def qpush(m):
+        return remote(q, qbuf.at[c], qs.at[m], qr.at[c], (lax.rem(chip + m, nk) * 2 + h, e))
+
+    qpair = remote(q, qbuf.at[c], qs.at[0], qr.at[c], (other, e))
+
+    def qrelay(m):
+        cs = asrc(2 * m)
+        return remote(qbuf.at[cs], qbuf.at[cs], qs.at[nk + m], qr.at[cs], (other, e))
+
+    qpair.start()
+    loop(nk, lambda m: qpush(m).start(), start=1)
 
     def gpush(j):
         return remote(gsend, gbuf.at[e], gs.at[j], gr.at[e], exp(j))
@@ -174,11 +185,11 @@
     kc = min(512, key_rows)
 
     def opush(j):
-        cs = csrc(j)
+        cs = asrc(j)
         return remote(osend.at[cs], obuf.at[c], os_.at[j], or_.at[c], (cs, e))
 
     def spush(j):
-        cs = csrc(j)
+        cs = asrc(j)
         return remote(stsend.at[cs], stbuf.at[c], ss.at[j], sr.at[c], (cs, e))
 
     def osend_start(j):
@@ -186,11 +197,15 @@
         opush(j).start()
 
     def attend(j):
-        cs = csrc(j)
+        cs = asrc(j)
 
         @pl.when(j > 0)
         def _():
             remote(q, qbuf.at[cs], qs.at[0], qr.at[cs], (cs, e)).wait_recv()
+
+        @pl.when((j > 0) & (lax.rem(j, 2) == 0))
+        def _():
+            qrelay(j // 2).start()
 
         @pl.when(j > 1)
         def _():
@@ -555,7 +570,10 @@
             f = i * 256 + hf * 128
             out[:, f : f + 128] = state[:, f : f + 128] + s[4 * hf : 4 * hf + 4, :]
 
-    for push in (qpush, opush, spush, gppush, hmpush, xpush, rpush):
+    qpair.wait_send()
+    for push in (qpush, qrelay):
+        loop(nk, lambda m, push=push: push(m).wait_send(), start=1)
+    for push in (opush, spush, gppush, hmpush, xpush, rpush):
         loop(cn, lambda j, push=push: push(j).wait_send(), start=1)
     for push in (gpush, ppush, epush, erelay):
         loop(en, lambda j, push=push: push(j).wait_send(), start=1)

time: 175 us -> 170 us (0.971)
  Pallas kernels: 171 us -> 166 us
    pallas_call x1, Pallas kernels: 171 us -> 166 us  [local(): pl.pallas_call(functools.partial(layer_kernel, cn, en), out_shape=(jax.Sh...]
where the time goes in v3:
time: 170 us
  Pallas kernels  166 us (98%)
  local copies, waits for them, and re-layouts  2.59 us (2%)
    pallas_call x1, Pallas kernels, local(): pl.pallas_call(functools.partial(layer_kernel, cn, en), out_shape=(jax.Sh...  166 us

profile of v3, /device:TPU:225, one launch (start us, length us, event | category | flops | bytes accessed | tf_op | source)
XLA Modules:
  0.0 169.7 jit_solution(4261387446809227978)
XLA Ops:
  0.6 166.5 %layer_kernel.1 = (f32[4,4096]{1,0:T(4,128)}, f32[1,4]{1,0:T(1,128)}) custom-call(bf16[64,512]{1,0:T(8,128)(2,1)} %q.1, bf16[2048,512]{1,0:T(8,128)(2,1)} %keys.1, bf16[2048,512]{1,0:T(8,128)(2,1)} %vals.1, bf16[2,256,3072]{2,1,0:T(8,128)(2,1)} %w.1, bf16[512,4096]{1,0:T(8,128)(2,1)} %outw.1, bf16[2,1536,256]{2,1,0:T(8,128)(2,1)} %wd.1, s32[4,8]{1,0:T(4,128)} %ids.1, ...), custom_call_target="tpu_custom_call" | custom-call | tf_op jit(solution)/shard_map/layer_kernel/pallas_call | solution.py:602
  167.1 1.5 copy.14
  168.6 1.1 copy.15

commit v4 on v3

--- a/solution.py
+++ b/solution.py
@@ -75,7 +75,7 @@
 def layer_kernel(cn, en, q, keys, vals, w, outw, wd, ids, gates, residual, gain, out, hm,
                  qbuf, kbuf, vbuf, vt, sbuf, mbuf, osend, obuf, stsend, stbuf, hmsend, hmbuf,
                  gsend, gbuf, gpsend, gall, owbuf, coef, a2, psend, pbuf, state, xsend, mid, xbuf,
-                 wbuf, slotm, gatem, xs, ysend, ybuf, hbuf, wdbuf, csend, r1, r2,
+                 wbuf, slotm, gatem, xs, ysend, ybuf, hbuf, wdbuf, csend, r1, rsum, r2,
                  qs, qr, os_, or_, ss, sr, ms, mr, gs, gr, gps, gpr, ws, wr, ps, pr, xsm, xrm,
                  es, er, es2, er2, ys, yr, hs, hr, hs2, hr2, cs_, cr_, rs_, rr_, ls):
     c, e = place(cn, en)
@@ -555,17 +555,19 @@
 
     def rpush(j):
         c2 = lax.rem(c + j, cn)
-        return remote(r1.at[:, c2], r2.at[c], rs_.at[j], rr_.at[c], (c2, e))
+        return remote(rsum.at[c2], r2.at[c], rs_.at[j], rr_.at[c], (c2, e))
 
     def rarrive(j):
         c2 = csrc(j)
-        remote(r1.at[:, c2], r2.at[c2], rs_.at[j], rr_.at[c2], (c2, e)).wait_recv()
-
+        remote(rsum.at[c2], r2.at[c2], rs_.at[j], rr_.at[c2], (c2, e)).wait_recv()
+
+    for i in range(cn):
+        rsum[i] = sum(r1[k, i].astype(F32) for k in range(en))
     loop(cn, lambda j: rpush(j).start(), start=1)
-    r2[c] = r1[:, c]
+    r2[c] = rsum[c]
     loop(cn, rarrive, start=1)
     for i in range(cn):
-        s = sum(r2[i, k].astype(F32) for k in range(en))
+        s = r2[i]
         for hf in range(2):
             f = i * 256 + hf * 128
             out[:, f : f + 128] = state[:, f : f + 128] + s[4 * hf : 4 * hf + 4, :]
@@ -643,7 +645,8 @@
             v((2, ff, fb), BF16),
             v((en, cn, 8, 128), BF16),
             v((en, cn, 8, 128), BF16),
-            v((cn, en, 8, 128), BF16),
+            v((cn, 8, 128), F32),
+            v((cn, 8, 128), F32),
             DMA((cn,)), DMA((cn,)), DMA((cn,)), DMA((cn,)), DMA((cn,)), DMA((cn,)),
             DMA((cn,)), DMA((cn,)), DMA((en,)), DMA((en,)), DMA((cn,)), DMA((cn,)),
             DMA((2,)), DMA((2,)), DMA((en,)), DMA((en,)), DMA((cn,)), DMA((cn,)),

time: 170 us -> 167 us (0.982)
  Pallas kernels: 166 us -> 163 us
    pallas_call x1, Pallas kernels: 166 us -> 163 us  [local(): pl.pallas_call(functools.partial(layer_kernel, cn, en), out_shape=(jax.Sh...]
where the time goes in v4:
time: 167 us
  Pallas kernels  163 us (98%)
  local copies, waits for them, and re-layouts  2.59 us (2%)
    pallas_call x1, Pallas kernels, local(): pl.pallas_call(functools.partial(layer_kernel, cn, en), out_shape=(jax.Sh...  163 us

profile of v4, /device:TPU:225, one launch (start us, length us, event | category | flops | bytes accessed | tf_op | source)
XLA Modules:
  0.0 166.6 jit_solution(8154897263163527318)
XLA Ops:
  0.6 163.3 %layer_kernel.1 = (f32[4,4096]{1,0:T(4,128)}, f32[1,4]{1,0:T(1,128)}) custom-call(bf16[64,512]{1,0:T(8,128)(2,1)} %q.1, bf16[2048,512]{1,0:T(8,128)(2,1)} %keys.1, bf16[2048,512]{1,0:T(8,128)(2,1)} %vals.1, bf16[2,256,3072]{2,1,0:T(8,128)(2,1)} %w.1, bf16[512,4096]{1,0:T(8,128)(2,1)} %outw.1, bf16[2,1536,256]{2,1,0:T(8,128)(2,1)} %wd.1, s32[4,8]{1,0:T(4,128)} %ids.1, ...), custom_call_target="tpu_custom_call" | custom-call | tf_op jit(solution)/shard_map/layer_kernel/pallas_call | solution.py:604
  164.0 1.5 copy.14
  165.5 1.1 copy.15
